TPU v7x, 32 devices: a whole 2x2x4 slice. The times are simulated.
32 devices in a mesh: wide: 8 (over z, x), narrow: 4 (over y, core).
Axes of the slice: x: 2, y: 2, z: 4, core: 2. Of those that a mesh axis runs over, the one named last changes fastest.
Arguments:
- tokens: bfloat16 [24, 512, 768], P('wide', 'narrow'), may hold values from -6 to 6
- lengths: int32 [24], P('wide'), may hold values from 1 to 512, as said below
- qkv_weight: bfloat16 [768, 2304], replicated, may hold values from -0.21875 to 0.21875
- qv_bias: float32 [2, 768], replicated, may hold values from -3 to 3
- out_weight: bfloat16 [768, 768], replicated, may hold values from -0.875 to 0.875
- out_bias: float32 [768], replicated, may hold values from -2 to 2
- norm1_gain: float32 [768], replicated, may hold values from 0.25 to 1.75
- norm1_shift: float32 [768], replicated, may hold values from -2 to 2
- up_weight: bfloat16 [768, 3072], replicated, may hold values from -0.21875 to 0.21875
- up_bias: float32 [3072], replicated, may hold values from -3 to 3
- down_weight: bfloat16 [3072, 768], replicated, may hold values from -0.109375 to 0.109375
- down_bias: float32 [768], replicated, may hold values from -2 to 2
- norm2_gain: float32 [768], replicated, may hold values from 0.25 to 1.75
- norm2_shift: float32 [768], replicated, may hold values from -2 to 2
- cotangent: bfloat16 [24, 512, 768], P('wide', 'narrow'), may hold values from -6 to 6
Outputs:
- output: bfloat16 [24, 512, 768], P('wide', 'narrow')
- input_grad: bfloat16 [24, 512, 768], P('wide', 'narrow')
- qkv_weight_grad: float32 [768, 2304], P('narrow')
- qv_bias_grad: float32 [2, 768], P(None, 'narrow')
- out_weight_grad: float32 [768, 768], P('narrow')
- out_bias_grad: float32 [768], P('narrow')
- norm1_gain_grad: float32 [768], P('narrow')
- norm1_shift_grad: float32 [768], P('narrow')
- up_weight_grad: float32 [768, 3072], P('narrow')
- up_bias_grad: float32 [3072], P('narrow')
- down_weight_grad: float32 [3072, 768], P('narrow')
- down_bias_grad: float32 [768], P('narrow')
- norm2_gain_grad: float32 [768], P('narrow')
- norm2_shift_grad: float32 [768], P('narrow')
Inputs may be any that keep to these rules, and one draw needn't show every extreme that they name: The slots of one group of 3 (aligned blocks) share a bucket b from 1 to 4, with lengths from (b - 1) * 128 + 1 to b * 128; slot 0 has length 512.
All inputs are finite; a program needn't handle non-finite values.
Results may differ from a plain program's by a relative error of at most 0.014.
Values may be sent and summed in bfloat16 or wider, within the bound.
A program may use at most 192 MiB of HBM per device.

v0:
```python
import jax
import jax.numpy as jnp
from jax import lax
from jax.sharding import PartitionSpec as P

H = 12
HD = 64
epsilon = 1e-12
root_half = 0.7071067811865476
inv_root_two_pi = 0.3989422804014327


def norm_forward(values, norm_gain, norm_shift):
    center = values - jnp.mean(values, axis=-1, keepdims=True)
    row_scale = lax.rsqrt(jnp.mean(center * center, axis=-1, keepdims=True) + epsilon)
    normed = center * row_scale
    return (normed * norm_gain + norm_shift, normed, row_scale)


def norm_backward(upstream, normed, row_scale, norm_gain):
    gain_grad = jnp.sum(upstream * normed, axis=0)
    shift_grad = jnp.sum(upstream, axis=0)
    scaled = upstream * norm_gain
    inner = scaled - jnp.mean(scaled, axis=-1, keepdims=True)
    inner = inner - normed * jnp.mean(scaled * normed, axis=-1, keepdims=True)
    return (row_scale * inner, gain_grad, shift_grad)


def split_packed(packed_seq):
    head_size = packed_seq.shape[2] // 3
    return (
        packed_seq[:, :, :head_size],
        packed_seq[:, :, head_size : 2 * head_size],
        packed_seq[:, :, 2 * head_size :],
    )


def masked_scores(query_part, key_part, length):
    raw_scores = jnp.einsum(
        "qhe,khe->hqk", query_part, key_part, preferred_element_type=jnp.float32
    )
    live_keys = lax.iota(jnp.int32, key_part.shape[0]) < length
    return jnp.where(live_keys[None, None, :], raw_scores * 0.125, -1000000000.0)


def attend(packed_seq, length):
    query_part, key_part, value_part = split_packed(packed_seq)
    scores = masked_scores(query_part, key_part, length)
    row_max = jnp.max(scores, axis=-1, keepdims=True)
    exponent = jnp.exp(scores - row_max)
    row_total = jnp.sum(exponent, axis=-1, keepdims=True)
    low_probs = (exponent / row_total).astype(jnp.bfloat16)
    context = jnp.einsum("hqk,khe->qhe", low_probs, value_part, preferred_element_type=jnp.float32)
    logsum = row_max + jnp.log(row_total)
    return (context.astype(jnp.bfloat16), logsum[:, :, 0])


def attend_backward(packed_seq, length, logsum, d_context):
    query_part, key_part, value_part = split_packed(packed_seq)
    scores = masked_scores(query_part, key_part, length)
    attn_probs = jnp.exp(scores - logsum[:, :, None])
    low_probs = attn_probs.astype(jnp.bfloat16)
    d_values = jnp.einsum("hqk,qhe->khe", low_probs, d_context, preferred_element_type=jnp.float32)
    d_probs = jnp.einsum("qhe,khe->hqk", d_context, value_part, preferred_element_type=jnp.float32)
    row_dot = jnp.sum(attn_probs * d_probs, axis=-1, keepdims=True)
    d_raw = (attn_probs * (d_probs - row_dot) * 0.125).astype(jnp.bfloat16)
    d_query = jnp.einsum("hqk,khe->qhe", d_raw, key_part, preferred_element_type=jnp.float32)
    d_keys = jnp.einsum("hqk,qhe->khe", d_raw, query_part, preferred_element_type=jnp.float32)
    return jnp.concatenate([d_query, d_keys, d_values], axis=-1).astype(jnp.bfloat16)


def local(
    tokens,
    lengths,
    qkv_weight,
    qv_bias,
    out_weight,
    out_bias,
    norm1_gain,
    norm1_shift,
    up_weight,
    up_bias,
    down_weight,
    down_bias,
    norm2_gain,
    norm2_shift,
    cotangent,
):
    groups, quarter, model_width = tokens.shape
    row_count = groups * quarter
    token_rows = tokens.reshape(row_count, model_width)
    zero_bias = jnp.zeros((H, HD), jnp.float32)
    bias_cols = jnp.stack([qv_bias[0].reshape(H, HD), zero_bias, qv_bias[1].reshape(H, HD)], axis=1)
    packed = jnp.dot(token_rows, qkv_weight, preferred_element_type=jnp.float32)
    packed = (packed + bias_cols.reshape(3 * model_width)).astype(jnp.bfloat16)
    packed = packed.reshape(groups, quarter, H, 3 * HD)
    head_parts = lax.all_to_all(packed, "narrow", split_axis=2, concat_axis=1, tiled=True)
    context, logsum = lax.map(lambda member: attend(member[0], member[1]), (head_parts, lengths))
    context_rows = lax.all_to_all(
        context, "narrow", split_axis=1, concat_axis=2, tiled=True
    ).reshape(row_count, model_width)
    attended = jnp.dot(context_rows, out_weight, preferred_element_type=jnp.float32) + out_bias
    first_norm, normed1, scale1 = norm_forward(
        token_rows.astype(jnp.float32) + attended, norm1_gain, norm1_shift
    )
    first_low = first_norm.astype(jnp.bfloat16)
    pre_act = jnp.dot(first_low, up_weight, preferred_element_type=jnp.float32) + up_bias
    erf_part = lax.erf(pre_act * root_half)
    activated = (0.5 * pre_act * (1.0 + erf_part)).astype(jnp.bfloat16)
    ffn_out = jnp.dot(activated, down_weight, preferred_element_type=jnp.float32) + down_bias
    result, normed2, scale2 = norm_forward(first_norm + ffn_out, norm2_gain, norm2_shift)
    output = result.astype(jnp.bfloat16).reshape(groups, quarter, model_width)
    positions = lax.axis_index("narrow") * quarter + lax.iota(jnp.int32, quarter)
    row_live = positions[None, :] < lengths[:, None]
    d_out = jnp.where(row_live[:, :, None], cotangent.astype(jnp.float32), 0.0).reshape(
        row_count, model_width
    )
    d_second, norm2_gain_grad, norm2_shift_grad = norm_backward(d_out, normed2, scale2, norm2_gain)
    d_ffn = d_second.astype(jnp.bfloat16)
    down_weight_grad = jnp.einsum("rf,rd->fd", activated, d_ffn, preferred_element_type=jnp.float32)
    down_bias_grad = jnp.sum(d_ffn.astype(jnp.float32), axis=0)
    d_activated = jnp.einsum("rd,fd->rf", d_ffn, down_weight, preferred_element_type=jnp.float32)
    slope = 0.5 * (1.0 + erf_part) + pre_act * jnp.exp(-0.5 * pre_act * pre_act) * inv_root_two_pi
    d_pre = (d_activated * slope).astype(jnp.bfloat16)
    up_weight_grad = jnp.einsum("rd,rf->df", first_low, d_pre, preferred_element_type=jnp.float32)
    up_bias_grad = jnp.sum(d_pre.astype(jnp.float32), axis=0)
    d_first = d_second + jnp.einsum(
        "rf,df->rd", d_pre, up_weight, preferred_element_type=jnp.float32
    )
    d_sum1, norm1_gain_grad, norm1_shift_grad = norm_backward(d_first, normed1, scale1, norm1_gain)
    d_att = d_sum1.astype(jnp.bfloat16)
    out_weight_grad = jnp.einsum(
        "rd,re->de", context_rows, d_att, preferred_element_type=jnp.float32
    )
    out_bias_grad = jnp.sum(d_att.astype(jnp.float32), axis=0)
    d_context = jnp.einsum("re,de->rd", d_att, out_weight, preferred_element_type=jnp.float32)
    d_context = d_context.astype(jnp.bfloat16).reshape(groups, quarter, H, HD)
    d_heads = lax.all_to_all(d_context, "narrow", split_axis=2, concat_axis=1, tiled=True)
    d_packed = lax.map(
        lambda member: attend_backward(member[0], member[1], member[2], member[3]),
        (head_parts, lengths, logsum, d_heads),
    )
    d_packed = lax.all_to_all(d_packed, "narrow", split_axis=1, concat_axis=2, tiled=True).reshape(
        row_count, 3 * model_width
    )
    qkv_weight_grad = jnp.einsum(
        "rd,rc->dc", token_rows, d_packed, preferred_element_type=jnp.float32
    )
    column_sums = jnp.sum(d_packed.astype(jnp.float32), axis=0).reshape(H, 3, HD)
    qv_bias_grad = jnp.stack(
        [column_sums[:, 0].reshape(model_width), column_sums[:, 2].reshape(model_width)]
    )
    d_input = d_sum1 + jnp.einsum(
        "rc,dc->rd", d_packed, qkv_weight, preferred_element_type=jnp.float32
    )
    input_grad = d_input.astype(jnp.bfloat16).reshape(groups, quarter, model_width)
    every_share = (
        lax.psum_scatter(qkv_weight_grad, "narrow", scatter_dimension=0, tiled=True),
        lax.psum_scatter(qv_bias_grad, "narrow", scatter_dimension=1, tiled=True),
        lax.psum_scatter(out_weight_grad, "narrow", scatter_dimension=0, tiled=True),
        lax.psum_scatter(out_bias_grad, "narrow", scatter_dimension=0, tiled=True),
        lax.psum_scatter(norm1_gain_grad, "narrow", scatter_dimension=0, tiled=True),
        lax.psum_scatter(norm1_shift_grad, "narrow", scatter_dimension=0, tiled=True),
        lax.psum_scatter(up_weight_grad, "narrow", scatter_dimension=0, tiled=True),
        lax.psum_scatter(up_bias_grad, "narrow", scatter_dimension=0, tiled=True),
        lax.psum_scatter(down_weight_grad, "narrow", scatter_dimension=0, tiled=True),
        lax.psum_scatter(down_bias_grad, "narrow", scatter_dimension=0, tiled=True),
        lax.psum_scatter(norm2_gain_grad, "narrow", scatter_dimension=0, tiled=True),
        lax.psum_scatter(norm2_shift_grad, "narrow", scatter_dimension=0, tiled=True),
    )
    every_total = lax.psum(
        (
            every_share[0],
            every_share[1],
            every_share[2],
            every_share[3],
            every_share[4],
            every_share[5],
            every_share[6],
            every_share[7],
            every_share[8],
            every_share[9],
            every_share[10],
            every_share[11],
        ),
        "wide",
    )
    return (
        output,
        input_grad,
        every_total[0],
        every_total[1],
        every_total[2],
        every_total[3],
        every_total[4],
        every_total[5],
        every_total[6],
        every_total[7],
        every_total[8],
        every_total[9],
        every_total[10],
        every_total[11],
    )


def solution(mesh):
    return jax.shard_map(
        local,
        mesh=mesh,
        in_specs=(
            P("wide", "narrow", None),
            P("wide"),
            P(),
            P(),
            P(),
            P(),
            P(),
            P(),
            P(),
            P(),
            P(),
            P(),
            P(),
            P(),
            P("wide", "narrow", None),
        ),
        out_specs=(
            P("wide", "narrow", None),
            P("wide", "narrow", None),
            P("narrow", None),
            P(None, "narrow"),
            P("narrow", None),
            P("narrow"),
            P("narrow"),
            P("narrow"),
            P("narrow", None),
            P("narrow"),
            P("narrow", None),
            P("narrow"),
            P("narrow"),
            P("narrow"),
        ),
        check_vma=False,
    )
```

profile of v0, /device:TPU:0, one launch (start us, length us, event | category | flops | bytes accessed | tf_op | source)
XLA Modules:
  0.0 858.6 jit_solution(15880051272732677894)
XLA Ops:
  30.0 22.8 %all-to-all-done = bf16[3,128,12,192]{1,3,0,2:T(8,128)(2,1)} async-done(((bf16[3,128,12,192]{1,3,0,2:T(8,128)(2,1)}), bf16[3,128,12,192]{1,3,0,2:T(8,128)(2,1)}, u32[]{:S(2)}, u32[]{:S(2)}) %all-to-all-start) | async-done | bytes 1769504 | tf_op jit(solution)/shard_map/all_to_all | solution.py:97
  60.9 18.2 %while.22 = (s32[]{:T(128)}, bf16[3,512,3,64]{1,3,2,0:T(8,128)(2,1)}, f32[3,3,512]{2,1,0:T(4,128)}, bf16[3,512,3,192]{1,3,2,0:T(8,128)(2,1)}, s32[3]{0:T(128)S(1)}, /*index=5*/s32[]{:T(128)}) while((s32[]{:T(128)}, bf16[3,512,3,64]{1,3,2,0:T(8,128)(2,1)}, f32[3,3,512]{2,1,0:T(4,128)}, bf16[3,512,3,192]{1,3,2,0:T(8,128)(2,1)}, s32[3]{0:T(128)S(1)}, ...), condition=%wide.region_3.4_spmd, body=%wide.region_0.3_spmd.sunk | while | flops 210861056 | bytes 11460713 | solution.py:98
  142.7 9.4 %all-to-all-done.2 = bf16[3,128,12,64]{1,3,0,2:T(8,128)(2,1)} async-done(((bf16[3,128,12,64]{1,3,0,2:T(8,128)(2,1)}), bf16[3,128,12,64]{1,3,0,2:T(8,128)(2,1)}, u32[]{:S(2)}, u32[]{:S(2)}) %all-to-all-start.2) | async-done | bytes 589856 | tf_op jit(solution)/shard_map/all_to_all | solution.py:138
  156.7 71.6 %while.23 = (s32[]{:T(128)}, bf16[3,512,3,192]{1,3,2,0:T(8,128)(2,1)}, bf16[3,512,3,192]{1,3,2,0:T(8,128)(2,1)}, s32[3]{0:T(128)}, f32[3,3,512]{2,1,0:T(4,128)}, /*index=5*/bf16[3,512,3,64]{1,3,2,0:T(8,128)(2,1)}, s32[]{:T(128)}) while((s32[]{:T(128)}, bf16[3,512,3,192]{1,3,2,0:T(8,128)(2,1)}, bf16[3,512,3,192]{1,3,2,0:T(8,128)(2,1)}, ...), condition=%wide.region_14.15_spmd, body=%wide.region_12.14_spmd.sunk | while | flops 516395520 | bytes 56251596 | solution.py:139
  165.7 6.4 fusion.147
  172.2 6.4 fusion.146
  189.6 6.4 fusion.147
  196.0 6.4 fusion.146
  213.4 6.4 fusion.147
  219.9 6.4 fusion.146
  233.8 42.2 %all_to_all.66 = bf16[3,512,3,192]{3,2,0,1:T(4,128)(2,1)} all-to-all(bf16[3,512,3,192]{3,2,0,1:T(4,128)(2,1)} %copy.77), channel_id=1, replica_groups=mesh['wide'=8,'narrow'=4] {'narrow'}, dimensions={1} | all-to-all | bytes 3538944 | tf_op jit(solution)/shard_map/all_to_all | solution.py:143
  276.0 7.2 copy.78
  283.2 6.7 convolution_bitcast_fusion
  289.9 8.0 copy.90
  301.8 9.9 %fusion.93 = f32[768,3072]{1,0:T(8,128)} fusion(bf16[384,3072]{1,0:T(8,128)(2,1)} %copy-done.10, f32[384,768]{1,0:T(8,128)} %copy-done.5, f32[768]{0:T(1024)S(1)} %copy-done.13, f32[768]{0:T(1024)S(1)} %copy-done.12, f32[384]{0:T(512)S(1)} %add_rsqrt_fusion.1, f32[384]{0:T(512)S(1)} %broadcast_multiply_fusion.4), kind=kOutput, calls=%fused_computation.130 | convolution fusion | flops 1813413888 | bytes 12985344 | tf_op jit(solution)/shard_map/rd,rf->df/dot_general | solution.py:125
  312.0 8.5 fusion.90
  320.6 7.5 convert_reduce_fusion.1
  332.1 30.8 %reduce-scatter.16.cloned.1.call-done = f32[192,2304]{1,0:T(8,128)} async-done(((f32[768,2304]{1,0:T(8,128)}), f32[192,2304]{1,0:T(8,128)}) %reduce-scatter.16.cloned.1.call-update) | async-done | bytes 1769488
  365.9 32.9 %reduce-scatter.10.cloned.1.call-done = f32[192,768]{1,0:T(8,128)} async-done(((f32[768,768]{1,0:T(8,128)}), f32[192,768]{1,0:T(8,128)}) %reduce-scatter.10.cloned.1.call-update) | async-done | bytes 589840 | tf_op jit(solution)/shard_map/reduce_scatter | solution.py:160
  398.7 81.1 %reduce-scatter.12.cloned.1.call-done = f32[192,3072]{1,0:T(8,128)} async-done(((f32[768,3072]{1,0:T(8,128)}), f32[192,3072]{1,0:T(8,128)}) %reduce-scatter.12.cloned.1.call-update) | async-done | bytes 2359312 | tf_op jit(solution)/shard_map/reduce_scatter | solution.py:164
  479.8 80.9 %reduce-scatter.14.cloned.1.call-done = f32[768,768]{1,0:T(8,128)} async-done(((f32[3072,768]{1,0:T(8,128)}), f32[768,768]{1,0:T(8,128)}) %reduce-scatter.14.cloned.1.call-update) | async-done | bytes 2359312 | tf_op jit(solution)/shard_map/reduce_scatter | solution.py:166
  563.3 11.1 %all-reduce.9 = (f32[768]{0:T(1024)}, f32[768]{0:T(1024)}, f32[768]{0:T(1024)}, f32[3072]{0:T(1024)}, f32[768]{0:T(1024)}, /*index=5*/f32[768]{0:T(1024)}, f32[768]{0:T(1024)}) all-reduce(f32[768]{0:T(1024)S(1)} %copy-done.19, f32[768]{0:T(1024)} %get-tuple-element.135, ...), channel_id=5, replica_groups=mesh['wide'=8,'narrow'=4] {'narrow'}, use_global_device_ids=true, to_apply=%region_23.24.clone | all-reduce | flops 7680 | bytes 61440
  587.3 38.8 %all-reduce.7 = (f32[2,192]{1,0:T(2,128)}, f32[192]{0:T(256)}, f32[192]{0:T(256)}, f32[192]{0:T(256)}, f32[768]{0:T(1024)}, /*index=5*/f32[192]{0:T(256)}, f32[192]{0:T(256)}, f32[192]{0:T(256)}) all-reduce(f32[2,192]{1,0:T(2,128)S(1)} %copy.93, f32[192]{0:T(256)S(1)} %dynamic-slice.1, ...), channel_id=1, replica_groups=mesh['wide'=8,'narrow'=4] {'wide'}, use_global_device_ids=true, to_apply=%region_19.20 | all-reduce | flops 2304 | bytes 18432 | tf_op jit(solution)/shard_map/psum | solution.py:171
  626.1 215.7 %all-reduce.12.cloned.1.call-done = (f32[192,2304]{0,1:T(8,128)}, f32[192,768]{1,0:T(8,128)}, f32[192,3072]{1,0:T(8,128)}, f32[768,768]{1,0:T(8,128)}) async-done(((f32[192,2304]{0,1:T(8,128)}, f32[192,768]{1,0:T(8,128)}, f32[192,3072]{1,0:T(8,128)}, f32[768,768]{1,0:T(8,128)}), (f32[192,2304]{0,1:T(8,128)}, f32[192,768]{1,0:T(8,128)}, f32[192,3072]{1,0:T(8,128)}, ...) | async-done | bytes 7077904 | tf_op jit(solution)/shard_map/psum | solution.py:171
  (203 shorter events, 190.3 us)
Async XLA Ops:
  7.2 3.9 copy-start
  25.4 4.6 copy-start.25
  25.4 27.4 %all-to-all-start = ((bf16[3,128,12,192]{1,3,0,2:T(8,128)(2,1)}), bf16[3,128,12,192]{1,3,0,2:T(8,128)(2,1)}, u32[]{:S(2)}, u32[]{:S(2)}) async-start(bf16[3,128,12,192]{1,3,0,2:T(8,128)(2,1)} %copy.68), calls=%async_computation | async-start | bytes 3538944 | tf_op jit(solution)/shard_map/all_to_all | solution.py:97
  82.5 8.5 copy-start.14
  86.4 14.2 %all-to-all-start.1 = ((bf16[4,2,36864]{2,1,0:T(2,128)(2,1)}), bf16[4,2,36864]{2,1,0:T(2,128)(2,1)}, u32[]{:S(2)}, u32[]{:S(2)}) async-start(bf16[4,2,36864]{2,1,0:T(2,128)(2,1)} %reshape.255), calls=%async_computation.1 | async-start | bytes 1179648 | tf_op jit(solution)/shard_map/all_to_all | solution.py:99
  94.6 14.0 %copy-start.23 = (f32[768]{0:T(1024)S(1)}, f32[768]{0:T(1024)}, u32[]{:S(2)}) copy-start(f32[768]{0:T(1024)} %param.24) | copy-start | bytes 9220
  108.5 7.3 slice-start
  111.1 18.2 %copy-start.5 = (f32[384,768]{1,0:T(8,128)}, f32[384,768]{1,0:T(8,128)S(1)}, u32[]{:S(2)}) copy-start(f32[384,768]{1,0:T(8,128)S(1)} %get-tuple-element.195) | copy-start | bytes 3538948
  111.5 4.5 slice-start.1
  111.5 4.4 copy-start.24
  120.4 6.0 slice-start.2
  122.4 4.1 copy-start.7
  122.4 4.1 slice-start.3
  138.3 13.8 %all-to-all-start.2 = ((bf16[3,128,12,64]{1,3,0,2:T(8,128)(2,1)}), bf16[3,128,12,64]{1,3,0,2:T(8,128)(2,1)}, u32[]{:S(2)}, u32[]{:S(2)}) async-start(bf16[3,128,12,64]{1,3,0,2:T(8,128)(2,1)} %copy.74), calls=%async_computation.2 | async-start | bytes 1179648 | tf_op jit(solution)/shard_map/all_to_all | solution.py:138
  142.5 220.4 %reduce-scatter.16.cloned.1.call-start = ((), (), s32[]{:S(2)}) async-start(), calls=%async_computation.12 | async-start | bytes 8847360
  160.4 3.0 copy-start.2
  184.2 3.0 copy-start.2
  208.1 3.0 copy-start.2
  298.0 100.8 %reduce-scatter.10.cloned.1.call-start = ((), (), s32[]{:S(2)}) async-start(), calls=%async_computation.9 | async-start | bytes 2949120 | tf_op jit(solution)/shard_map/reduce_scatter | solution.py:160
  301.7 178.1 %reduce-scatter.12.cloned.1.call-start = ((), (), s32[]{:S(2)}) async-start(), calls=%async_computation.10 | async-start | bytes 11796480 | tf_op jit(solution)/shard_map/reduce_scatter | solution.py:164
  311.7 249.0 %reduce-scatter.14.cloned.1.call-start = ((), (), s32[]{:S(2)}) async-start(), calls=%async_computation.11 | async-start | bytes 11796480 | tf_op jit(solution)/shard_map/reduce_scatter | solution.py:166
  320.6 265.8 %reduce-scatter.18.cloned.1.call-start = ((), (), s32[]{:S(2)}) async-start(), calls=%async_computation.13 | async-start | bytes 491520
  332.1 509.8 %all-reduce.12.cloned.1.call-start = ((), (), s32[]{:S(2)}) async-start(), calls=%async_computation.14 | async-start | bytes 15335424 | tf_op jit(solution)/shard_map/psum | solution.py:171
  846.6 3.5 copy-start.9
  (21 other events, 44.8 us)
Sparse Core Ops, SparseCore 0:
  298.1 64.7 reduce-scatter.15
  365.6 33.0 reduce-scatter.9
  401.3 78.4 reduce-scatter.11
  482.3 78.3 reduce-scatter.13
  563.6 20.7 reduce-scatter.17
  589.4 252.3 all-reduce.11
where the time goes:
time: 867 us; the launch traced here: 859 us
  waiting for transfers between devices  480 us (55%)
  matrix products  115 us (13%)
  local copies, waits for them, and re-layouts  111 us (13%)
  blocking collectives  92.1 us (11%)
  other arithmetic  30 us (3%)
  between operations  16 us (2%)
  starting transfers between devices  13.9 us (2%)
    psum x1, waiting for transfers between devices, local(): lax.psum((every_share[0], every_share[1], every_share[2], every_share[3],...  216 us
    reduce_scatter x1, waiting for transfers between devices, local(): lax.psum_scatter(up_weight_grad, 'narrow', scatter_dimension=0, tiled=True)  81.1 us
    reduce_scatter x1, waiting for transfers between devices, local(): lax.psum_scatter(down_weight_grad, 'narrow', scatter_dimension=0, tiled=T...  80.9 us
    all_to_all x1, blocking collectives, local(): lax.all_to_all(d_packed, 'narrow', split_axis=1, concat_axis=2, tiled=True)  42.2 us
    unnamed x72, local copies, waits for them, and re-layouts  41.2 us
    psum x1, blocking collectives, local(): lax.psum((every_share[0], every_share[1], every_share[2], every_share[3],...  38.8 us
    reduce_scatter x1, waiting for transfers between devices, local(): lax.psum_scatter(out_weight_grad, 'narrow', scatter_dimension=0, tiled=True)  32.9 us
    unnamed x8, waiting for transfers between devices  30.9 us
  transfers between devices with their start and end apart: 9, of which 8 were waited for; matrix products, arithmetic and copies ran while one was open for 6% of the time, Pallas kernels for 0%

commit v1 on v0

--- a/solution.py
+++ b/solution.py
@@ -1,3 +1,4 @@
+import functools
 import jax
 import jax.numpy as jnp
 from jax import lax
@@ -8,6 +9,40 @@
 epsilon = 1e-12
 root_half = 0.7071067811865476
 inv_root_two_pi = 0.3989422804014327
+
+
+def get_rings_over_axis(x0, out_dim, own_rows):
+    mixed_arr = x0.shape
+    new = x0.reshape(
+        *mixed_arr[:out_dim], own_rows, mixed_arr[out_dim] // own_rows, *mixed_arr[out_dim + 1 :]
+    )
+    return jnp.moveaxis(new, out_dim, 0)
+
+
+def launch_routes_all_on(block_in, dim_no):
+    long_array = list(block_in.shape[1:])
+    long_array[dim_no] *= block_in.shape[0]
+    return jnp.moveaxis(block_in, 0, dim_no).reshape(long_array)
+
+
+def _run_lanes(obj, ax_name, piece_in, body):
+    k_now = lax.psum(1, ax_name)
+    last = lax.axis_index(ax_name)
+    before, side_arr = (k_now, last)
+    u_next = get_rings_over_axis(obj, piece_in, before)
+    panels = [u_next[side_arr]]
+    q = 1
+    while q < before:
+        outer = u_next[side_arr ^ q]
+        current_value = lax.ppermute(outer, ax_name, perm=[(u, u ^ q) for u in range(before)])
+        panels.append(current_value)
+        q += 1
+    formed = jnp.stack(panels, 0)
+    u_next = formed[side_arr ^ jnp.arange(before)]
+    return launch_routes_all_on(u_next, body)
+
+
+balance_object = functools.partial(_run_lanes, ax_name="narrow", piece_in=2, body=1)
 
 
 def norm_forward(values, norm_gain, norm_shift):
@@ -135,7 +170,7 @@
     out_bias_grad = jnp.sum(d_att.astype(jnp.float32), axis=0)
     d_context = jnp.einsum("re,de->rd", d_att, out_weight, preferred_element_type=jnp.float32)
     d_context = d_context.astype(jnp.bfloat16).reshape(groups, quarter, H, HD)
-    d_heads = lax.all_to_all(d_context, "narrow", split_axis=2, concat_axis=1, tiled=True)
+    d_heads = balance_object(d_context)
     d_packed = lax.map(
         lambda member: attend_backward(member[0], member[1], member[2], member[3]),
         (head_parts, lengths, logsum, d_heads),

time: 867 us -> 868 us (level)
    all_to_all x1 -> x0, waiting for transfers between devices: 9.38 us -> none  [local(): lax.all_to_all(d_context, 'narrow', split_axis=2, concat_axis=1, tiled=True)]
  transfers between devices with their start and end apart: 9 -> 11, of which waited for: 8 -> 9; matrix products, arithmetic and copies ran while one was open for 6% -> 7% of each run, Pallas kernels for 0% -> 0%
where the time goes in v1:
time: 868 us; the launch traced here: 859 us
  waiting for transfers between devices  475 us (55%)
  local copies, waits for them, and re-layouts  116 us (13%)
  matrix products  115 us (13%)
  blocking collectives  92.1 us (11%)
  other arithmetic  33.7 us (4%)
  between operations  16.1 us (2%)
  starting transfers between devices  11.5 us (1%)
    psum x1, waiting for transfers between devices, local(): lax.psum((every_share[0], every_share[1], every_share[2], every_share[3],...  216 us
    reduce_scatter x1, waiting for transfers between devices, local(): lax.psum_scatter(up_weight_grad, 'narrow', scatter_dimension=0, tiled=True)  81.1 us
    reduce_scatter x1, waiting for transfers between devices, local(): lax.psum_scatter(down_weight_grad, 'narrow', scatter_dimension=0, tiled=T...  80.9 us
    all_to_all x1, blocking collectives, local(): lax.all_to_all(d_packed, 'narrow', split_axis=1, concat_axis=2, tiled=True)  42.2 us
    unnamed x72, local copies, waits for them, and re-layouts  41.2 us
    psum x1, blocking collectives, local(): lax.psum((every_share[0], every_share[1], every_share[2], every_share[3],...  38.8 us
    reduce_scatter x1, waiting for transfers between devices, local(): lax.psum_scatter(out_weight_grad, 'narrow', scatter_dimension=0, tiled=True)  32.9 us
    unnamed x8, waiting for transfers between devices  30.9 us
  transfers between devices with their start and end apart: 11, of which 9 were waited for; matrix products, arithmetic and copies ran while one was open for 7% of the time, Pallas kernels for 0%

profile of v1, /device:TPU:0, one launch (start us, length us, event | category | flops | bytes accessed | tf_op | source)
XLA Modules:
  0.0 859.4 jit_solution(7734831447610549822)
XLA Ops:
  14.9 5.8 reshape.268
  30.1 22.8 %all-to-all-done = bf16[3,128,12,192]{1,3,0,2:T(8,128)(2,1)} async-done(((bf16[3,128,12,192]{1,3,0,2:T(8,128)(2,1)}), bf16[3,128,12,192]{1,3,0,2:T(8,128)(2,1)}, u32[]{:S(2)}, u32[]{:S(2)}) %all-to-all-start) | async-done | bytes 1769504 | tf_op jit(solution)/shard_map/all_to_all | solution.py:132
  60.9 18.2 %while.22 = (s32[]{:T(128)}, bf16[3,512,3,64]{1,3,2,0:T(8,128)(2,1)}, f32[3,3,512]{2,1,0:T(4,128)}, bf16[3,512,3,192]{1,3,2,0:T(8,128)(2,1)}, s32[3]{0:T(128)S(1)}, /*index=5*/s32[]{:T(128)}) while((s32[]{:T(128)}, bf16[3,512,3,64]{1,3,2,0:T(8,128)(2,1)}, f32[3,3,512]{2,1,0:T(4,128)}, bf16[3,512,3,192]{1,3,2,0:T(8,128)(2,1)}, s32[3]{0:T(128)S(1)}, ...), condition=%wide.region_3.4_spmd, body=%wide.region_0.3_spmd.sunk | while | flops 210861056 | bytes 11460713 | solution.py:133
  157.3 71.7 %while.23 = (s32[]{:T(128)}, bf16[3,512,3,192]{1,3,2,0:T(8,128)(2,1)}, bf16[3,512,3,192]{1,3,2,0:T(8,128)(2,1)}, s32[3]{0:T(128)}, f32[3,3,512]{2,1,0:T(4,128)}, /*index=5*/bf16[3,512,3,64]{1,3,2,0:T(8,128)(2,1)}, s32[]{:T(128)}) while((s32[]{:T(128)}, bf16[3,512,3,192]{1,3,2,0:T(8,128)(2,1)}, bf16[3,512,3,192]{1,3,2,0:T(8,128)(2,1)}, ...), condition=%wide.region_14.15_spmd, body=%wide.region_12.14_spmd.sunk | while | flops 516395520 | bytes 56251596 | solution.py:174
  166.5 6.4 fusion.149
  173.0 6.4 fusion.148
  190.4 6.4 fusion.149
  196.8 6.4 fusion.148
  214.2 6.4 fusion.149
  220.7 6.4 fusion.148
  234.6 42.2 %all_to_all.48 = bf16[3,512,3,192]{3,2,0,1:T(4,128)(2,1)} all-to-all(bf16[3,512,3,192]{3,2,0,1:T(4,128)(2,1)} %copy.84), channel_id=1, replica_groups=mesh['wide'=8,'narrow'=4] {'narrow'}, dimensions={1} | all-to-all | bytes 3538944 | tf_op jit(solution)/shard_map/all_to_all | solution.py:178
  276.8 7.2 copy.85
  284.0 6.7 convolution_bitcast_fusion
  290.7 8.0 copy.94
  302.6 9.9 %fusion.94 = f32[768,3072]{1,0:T(8,128)} fusion(bf16[384,3072]{1,0:T(8,128)(2,1)} %copy-done.10, f32[384,768]{1,0:T(8,128)} %copy-done.5, f32[768]{0:T(1024)S(1)} %copy-done.13, f32[768]{0:T(1024)S(1)} %copy-done.12, f32[384]{0:T(512)S(1)} %add_rsqrt_fusion.1, f32[384]{0:T(512)S(1)} %broadcast_multiply_fusion.4), kind=kOutput, calls=%fused_computation.144 | convolution fusion | flops 1813413888 | bytes 12985344 | tf_op jit(solution)/shard_map/rd,rf->df/dot_general | solution.py:160
  312.8 8.5 fusion.91
  321.4 7.5 convert_reduce_fusion.1
  332.9 30.8 %reduce-scatter.16.cloned.1.call-done = f32[192,2304]{1,0:T(8,128)} async-done(((f32[768,2304]{1,0:T(8,128)}), f32[192,2304]{1,0:T(8,128)}) %reduce-scatter.16.cloned.1.call-update) | async-done | bytes 1769488
  366.7 32.9 %reduce-scatter.10.cloned.1.call-done = f32[192,768]{1,0:T(8,128)} async-done(((f32[768,768]{1,0:T(8,128)}), f32[192,768]{1,0:T(8,128)}) %reduce-scatter.10.cloned.1.call-update) | async-done | bytes 589840 | tf_op jit(solution)/shard_map/reduce_scatter | solution.py:195
  399.5 81.1 %reduce-scatter.12.cloned.1.call-done = f32[192,3072]{1,0:T(8,128)} async-done(((f32[768,3072]{1,0:T(8,128)}), f32[192,3072]{1,0:T(8,128)}) %reduce-scatter.12.cloned.1.call-update) | async-done | bytes 2359312 | tf_op jit(solution)/shard_map/reduce_scatter | solution.py:199
  480.6 80.9 %reduce-scatter.14.cloned.1.call-done = f32[768,768]{1,0:T(8,128)} async-done(((f32[3072,768]{1,0:T(8,128)}), f32[768,768]{1,0:T(8,128)}) %reduce-scatter.14.cloned.1.call-update) | async-done | bytes 2359312 | tf_op jit(solution)/shard_map/reduce_scatter | solution.py:201
  564.1 11.1 %all-reduce.9 = (f32[768]{0:T(1024)}, f32[768]{0:T(1024)}, f32[768]{0:T(1024)}, f32[3072]{0:T(1024)}, f32[768]{0:T(1024)}, /*index=5*/f32[768]{0:T(1024)}, f32[768]{0:T(1024)}) all-reduce(f32[768]{0:T(1024)S(1)} %copy-done.19, f32[768]{0:T(1024)} %get-tuple-element.135, ...), channel_id=5, replica_groups=mesh['wide'=8,'narrow'=4] {'narrow'}, use_global_device_ids=true, to_apply=%region_23.24.clone | all-reduce | flops 7680 | bytes 61440
  588.1 38.8 %all-reduce.7 = (f32[2,192]{1,0:T(2,128)}, f32[192]{0:T(256)}, f32[192]{0:T(256)}, f32[192]{0:T(256)}, f32[768]{0:T(1024)}, /*index=5*/f32[192]{0:T(256)}, f32[192]{0:T(256)}, f32[192]{0:T(256)}) all-reduce(f32[2,192]{1,0:T(2,128)S(1)} %copy.97, f32[192]{0:T(256)S(1)} %dynamic-slice.17, ...), channel_id=1, replica_groups=mesh['wide'=8,'narrow'=4] {'wide'}, use_global_device_ids=true, to_apply=%region_19.20 | all-reduce | flops 2304 | bytes 18432 | tf_op jit(solution)/shard_map/psum | solution.py:206
  626.9 215.7 %all-reduce.12.cloned.1.call-done = (f32[192,2304]{0,1:T(8,128)}, f32[192,768]{1,0:T(8,128)}, f32[192,3072]{1,0:T(8,128)}, f32[768,768]{1,0:T(8,128)}) async-done(((f32[192,2304]{0,1:T(8,128)}, f32[192,768]{1,0:T(8,128)}, f32[192,3072]{1,0:T(8,128)}, f32[768,768]{1,0:T(8,128)}), (f32[192,2304]{0,1:T(8,128)}, f32[192,768]{1,0:T(8,128)}, f32[192,3072]{1,0:T(8,128)}, ...) | async-done | bytes 7077904 | tf_op jit(solution)/shard_map/psum | solution.py:206
  (215 shorter events, 194.5 us)
Async XLA Ops:
  7.2 3.9 copy-start
  25.4 4.6 copy-start.25
  25.4 27.4 %all-to-all-start = ((bf16[3,128,12,192]{1,3,0,2:T(8,128)(2,1)}), bf16[3,128,12,192]{1,3,0,2:T(8,128)(2,1)}, u32[]{:S(2)}, u32[]{:S(2)}) async-start(bf16[3,128,12,192]{1,3,0,2:T(8,128)(2,1)} %copy.73), calls=%async_computation | async-start | bytes 3538944 | tf_op jit(solution)/shard_map/all_to_all | solution.py:132
  82.5 8.6 copy-start.14
  86.4 13.8 %all-to-all-start.1 = ((bf16[4,2,36864]{2,1,0:T(2,128)(2,1)}), bf16[4,2,36864]{2,1,0:T(2,128)(2,1)}, u32[]{:S(2)}, u32[]{:S(2)}) async-start(bf16[4,2,36864]{2,1,0:T(2,128)(2,1)} %reshape.285), calls=%async_computation.1 | async-start | bytes 1179648 | tf_op jit(solution)/shard_map/all_to_all | solution.py:134
  90.6 273.2 %reduce-scatter.16.cloned.1.call-start = ((), (), s32[]{:S(2)}) async-start(), calls=%async_computation.11 | async-start | bytes 8847360
  94.6 13.5 %copy-start.23 = (f32[768]{0:T(1024)S(1)}, f32[768]{0:T(1024)}, u32[]{:S(2)}) copy-start(f32[768]{0:T(1024)} %param.24) | copy-start | bytes 9220
  108.1 7.3 slice-start
  110.7 18.2 %copy-start.5 = (f32[384,768]{1,0:T(8,128)}, f32[384,768]{1,0:T(8,128)S(1)}, u32[]{:S(2)}) copy-start(f32[384,768]{1,0:T(8,128)S(1)} %get-tuple-element.199) | copy-start | bytes 3538948
  111.0 4.5 slice-start.1
  111.0 4.4 copy-start.24
  120.0 6.0 slice-start.2
  121.9 4.1 copy-start.7
  121.9 4.1 slice-start.3
  141.4 4.6 collective-permute-start
  141.4 7.0 collective-permute-start.1
  141.8 9.0 %collective-permute-start.2 = (bf16[3,128,3,64]{1,3,2,0:T(8,128)(2,1)}, bf16[3,128,3,64]{1,3,2,0:T(8,128)(2,1)}, u32[]{:S(2)}, u32[]{:S(2)}) collective-permute-start(bf16[3,128,3,64]{1,3,2,0:T(8,128)(2,1)} %bitcast.126), channel_id=1, source_target_pairs={{0,3},{1,2},{2,1},{3,0},{4,7},{5,6},{6,5},{7,4},{8,11},{9,10},{10,... | collective-permute-start | bytes 442376 | tf_op jit(solution)/shard_map/ppermute | solution.py:37
  185.0 3.0 copy-start.2
  298.8 100.8 %reduce-scatter.10.cloned.1.call-start = ((), (), s32[]{:S(2)}) async-start(), calls=%async_computation.8 | async-start | bytes 2949120 | tf_op jit(solution)/shard_map/reduce_scatter | solution.py:195
  302.5 178.1 %reduce-scatter.12.cloned.1.call-start = ((), (), s32[]{:S(2)}) async-start(), calls=%async_computation.9 | async-start | bytes 11796480 | tf_op jit(solution)/shard_map/reduce_scatter | solution.py:199
  312.5 249.0 %reduce-scatter.14.cloned.1.call-start = ((), (), s32[]{:S(2)}) async-start(), calls=%async_computation.10 | async-start | bytes 11796480 | tf_op jit(solution)/shard_map/reduce_scatter | solution.py:201
  321.4 265.8 %reduce-scatter.18.cloned.1.call-start = ((), (), s32[]{:S(2)}) async-start(), calls=%async_computation.12 | async-start | bytes 491520
  332.9 509.8 %all-reduce.12.cloned.1.call-start = ((), (), s32[]{:S(2)}) async-start(), calls=%async_computation.13 | async-start | bytes 15335424 | tf_op jit(solution)/shard_map/psum | solution.py:206
  847.4 3.5 copy-start.9
  (23 other events, 50.8 us)
Sparse Core Ops, SparseCore 0:
  298.9 64.7 reduce-scatter.15
  366.4 33.0 reduce-scatter.9
  402.1 78.4 reduce-scatter.11
  483.1 78.3 reduce-scatter.13
  564.4 20.7 reduce-scatter.17
  590.2 252.3 all-reduce.11
